TPU v7x, 32 devices: a whole 2x2x4 slice. The times are simulated.
32 devices in a mesh: parts: 2 (over y), turn: 4 (over x, core), branch: 4 (over z).
Axes of the slice: x: 2, y: 2, z: 4, core: 2. Of those that a mesh axis runs over, the one named last changes fastest.
Arguments:
- query: bfloat16 [4096, 4096], P(('parts', 'turn', 'branch')), parts along dimension 0, may hold values from -128 to 128
- branch_key_value: bfloat16 [2, 4096, 512], P(None, ('parts', 'turn', 'branch')), parts along dimension 1, may hold values from -4 to 4
- turn_key_value: bfloat16 [2, 64, 512], P(None, ('parts', 'turn', 'branch')), parts along dimension 1, may hold values from -4 to 4
- kv_trunk: bfloat16 [2, 32, 512], P(None, ('parts', 'turn', 'branch')), parts along dimension 1, may hold values from -4 to 4
- grad_out: bfloat16 [4096, 4096], P(('parts', 'turn', 'branch')), parts along dimension 0, may hold values from -6 to 6
- branch_lengths: int32 [32, 4], P(('parts', 'turn', 'branch')), parts along dimension 0, may hold values from 1 to 64, 128 in all within a row
- parents: int32 [8], P('parts'), parts along dimension 0, may hold values from -1 to 2, as said below
Outputs:
- attended: bfloat16 [4096, 4096], P(('parts', 'turn', 'branch')), parts along dimension 0
- grad_query: bfloat16 [4096, 4096], P(('parts', 'turn', 'branch')), parts along dimension 0
- grad_branch_kv: bfloat16 [2, 4096, 512], P(None, ('parts', 'turn', 'branch')), parts along dimension 1
- grad_turn_kv: bfloat16 [2, 64, 512], P(None, ('parts', 'turn', 'branch')), parts along dimension 1
- grad_trunk_kv: bfloat16 [2, 32, 512], P(None, ('parts', 'turn', 'branch')), parts along dimension 1
There are 2 independent parts, one for each index of `parts`. A program takes and returns all parts, laid end to end along the dimension named above; each array names one. Nothing has to cross between parts.
Inputs may be any that keep to these rules, and one draw needn't show every extreme that they name: parents[t] is -1 or a turn before t; parents[0] is -1 and the last turn's parent is the turn before it.
All inputs are finite; a program needn't handle non-finite values.
Results may differ from a plain program's by a relative error of at most 0.02.
Values may be sent and summed in bfloat16 or wider, within the bound.
A program may use at most 64 MiB of HBM per device.

v0:
```python
import math

import jax
import jax.numpy as jnp
from jax import lax
from jax.sharding import PartitionSpec as P

QUERY_HEADS = 32
KEY_VALUE_HEADS = 4
HEAD_SIZE = 128
QUERY_PER_KEY = 8


masked_score = -1e30


def ancestry(parents, turn_count):
    position = jnp.arange(turn_count, dtype=jnp.int32)
    parent_of = parents[:, None] == position[None, :]
    start = position[:, None] == position[None, :]

    def widen(sweep, reached):
        return reached | jnp.any(reached[:, :, None] & parent_of[None, :, :], axis=1)

    return lax.fori_loop(0, turn_count, widen, start)


def visible(path_row, lengths, trunk_rows, turn_rows, turn_count, branch_rows):
    turn_length = turn_rows // turn_count
    owner_turn = jnp.arange(turn_rows, dtype=jnp.int32) // turn_length
    on_path = jnp.any(
        (owner_turn[:, None] == jnp.arange(turn_count, dtype=jnp.int32)[None, :])
        & path_row[None, :],
        axis=1,
    )
    segment_ends = jnp.cumsum(lengths, dtype=jnp.int32)
    position = jnp.arange(branch_rows, dtype=jnp.int32)
    segment = jnp.sum((position[:, None] >= segment_ends[None, :]).astype(jnp.int32), axis=1)
    inside = (segment[:, None] == segment[None, :]) & (position[None, :] <= position[:, None])
    leading = jnp.ones((branch_rows, trunk_rows), dtype=bool)
    middle = jnp.broadcast_to(on_path[None, :], (branch_rows, turn_rows))
    return jnp.concatenate([leading, middle, inside], axis=1)


def group_terms(query, key_rows, values, grad_out, allowed, group_index):
    query_total = query.shape[0]
    group_width = QUERY_PER_KEY * HEAD_SIZE
    softmax_scale = 1.0 / math.sqrt(HEAD_SIZE)
    start = group_index * group_width
    queries = lax.dynamic_slice_in_dim(query, start, group_width, 1).reshape(
        query_total, QUERY_PER_KEY, HEAD_SIZE
    )
    cotangent = lax.dynamic_slice_in_dim(grad_out, start, group_width, 1).reshape(
        query_total, QUERY_PER_KEY, HEAD_SIZE
    )
    head_keys = lax.dynamic_slice_in_dim(key_rows, group_index * HEAD_SIZE, HEAD_SIZE, 1)
    head_values = lax.dynamic_slice_in_dim(values, group_index * HEAD_SIZE, HEAD_SIZE, 1)
    scores = (
        jnp.einsum("rgd,kd->grk", queries, head_keys, preferred_element_type=jnp.float32)
        * softmax_scale
    )
    scores = jnp.where(allowed[None, :, :], scores, masked_score)
    largest = jnp.max(scores, axis=2, keepdims=True)
    exponent = jnp.exp(scores - largest)
    probs = exponent / jnp.sum(exponent, axis=2, keepdims=True)
    rounded = probs.astype(jnp.bfloat16)
    attended = jnp.einsum(
        "grk,kd->rgd", rounded, head_values, preferred_element_type=jnp.float32
    ).astype(jnp.bfloat16)
    delta = jnp.sum(cotangent.astype(jnp.float32) * attended.astype(jnp.float32), axis=2)
    dprob = jnp.einsum("rgd,kd->grk", cotangent, head_values, preferred_element_type=jnp.float32)
    dscore = (probs * (dprob - jnp.transpose(delta)[:, :, None])).astype(jnp.bfloat16)
    grad_query = (
        jnp.einsum("grk,kd->rgd", dscore, head_keys, preferred_element_type=jnp.float32)
        * softmax_scale
    ).astype(jnp.bfloat16)
    grad_keys = (
        jnp.einsum("grk,rgd->kd", dscore, queries, preferred_element_type=jnp.float32)
        * softmax_scale
    )
    grad_values = jnp.einsum("grk,rgd->kd", rounded, cotangent, preferred_element_type=jnp.float32)
    return (
        attended.reshape(query_total, group_width),
        grad_query.reshape(query_total, group_width),
        grad_keys,
        grad_values,
    )


def device_terms(query, key_rows, values, grad_out, allowed):
    query_total = query.shape[0]
    key_total = key_rows.shape[0]
    group_width = QUERY_PER_KEY * HEAD_SIZE

    def single_group(group_index, totals):
        attended, grad_query, grad_keys, grad_values = totals
        piece_out, piece_query, piece_keys, piece_values = group_terms(
            query, key_rows, values, grad_out, allowed, group_index
        )
        attended = lax.dynamic_update_slice_in_dim(
            attended, piece_out, group_index * group_width, 1
        )
        grad_query = lax.dynamic_update_slice_in_dim(
            grad_query, piece_query, group_index * group_width, 1
        )
        grad_keys = lax.dynamic_update_slice_in_dim(
            grad_keys, piece_keys, group_index * HEAD_SIZE, 1
        )
        grad_values = lax.dynamic_update_slice_in_dim(
            grad_values, piece_values, group_index * HEAD_SIZE, 1
        )
        return (attended, grad_query, grad_keys, grad_values)

    initial_state = (
        jnp.zeros((query_total, QUERY_HEADS * HEAD_SIZE), jnp.bfloat16),
        jnp.zeros((query_total, QUERY_HEADS * HEAD_SIZE), jnp.bfloat16),
        jnp.zeros((key_total, KEY_VALUE_HEADS * HEAD_SIZE), jnp.float32),
        jnp.zeros((key_total, KEY_VALUE_HEADS * HEAD_SIZE), jnp.float32),
    )
    return lax.fori_loop(0, KEY_VALUE_HEADS, single_group, initial_state)


def on_device(query, branch_key_value, turn_key_value, kv_trunk, grad_out, branch_lengths, parents):
    turn_count = lax.axis_size("turn")
    nearby = (
        lax.all_gather(kv_trunk, "branch", axis=1, tiled=True),
        lax.all_gather(turn_key_value, "branch", axis=1, tiled=True),
    )
    trunk_all, turn_all = (
        lax.all_gather(nearby[0], "turn", axis=1, tiled=True),
        lax.all_gather(nearby[1], "turn", axis=1, tiled=True),
    )
    reached = ancestry(parents, turn_count)
    turn_index = lax.axis_index("turn")
    path_row = jnp.any(
        reached & (jnp.arange(turn_count, dtype=jnp.int32)[:, None] == turn_index), axis=0
    )
    trunk_rows = trunk_all.shape[1]
    turn_rows = turn_all.shape[1]
    shared_rows = trunk_rows + turn_rows
    allowed = visible(
        path_row, branch_lengths[0], trunk_rows, turn_rows, turn_count, query.shape[0]
    )
    key_rows = jnp.concatenate([trunk_all[0], turn_all[0], branch_key_value[0]], axis=0)
    value_rows = jnp.concatenate([trunk_all[1], turn_all[1], branch_key_value[1]], axis=0)
    attended, grad_query, grad_keys, grad_values = device_terms(
        query, key_rows, value_rows, grad_out, allowed
    )
    grad_trunk = jnp.stack([grad_keys[:trunk_rows], grad_values[:trunk_rows]])
    grad_turn = jnp.stack([grad_keys[trunk_rows:shared_rows], grad_values[trunk_rows:shared_rows]])
    grad_branch = jnp.stack([grad_keys[shared_rows:], grad_values[shared_rows:]]).astype(
        jnp.bfloat16
    )
    sum_trunk, sum_turn = (
        lax.psum_scatter(grad_trunk, ("turn", "branch"), scatter_dimension=1, tiled=True),
        lax.psum_scatter(grad_turn, ("turn", "branch"), scatter_dimension=1, tiled=True),
    )
    return (
        attended,
        grad_query,
        grad_branch,
        sum_turn.astype(jnp.bfloat16),
        sum_trunk.astype(jnp.bfloat16),
    )


def solution(mesh):
    return jax.shard_map(
        on_device,
        mesh=mesh,
        in_specs=(
            P(("parts", "turn", "branch"), None),
            P(None, ("parts", "turn", "branch"), None),
            P(None, ("parts", "turn", "branch"), None),
            P(None, ("parts", "turn", "branch"), None),
            P(("parts", "turn", "branch"), None),
            P(("parts", "turn", "branch"), None),
            P("parts"),
        ),
        out_specs=(
            P(("parts", "turn", "branch"), None),
            P(("parts", "turn", "branch"), None),
            P(None, ("parts", "turn", "branch"), None),
            P(None, ("parts", "turn", "branch"), None),
            P(None, ("parts", "turn", "branch"), None),
        ),
        check_vma=False,
    )
```

profile of v0, /device:TPU:0, one launch (start us, length us, event | category | flops | bytes accessed | tf_op | source)
XLA Modules:
  0.0 157.0 jit_solution(16002256091089100070)
XLA Ops:
  2.6 0.6 copy-done.11
  3.5 0.6 copy-done.12
  4.1 0.8 while.31
  5.6 0.7 copy-done.10
  6.3 13.6 %all_gather.12 = bf16[2,4,512]{2,0,1:T(2,128)(2,1)S(1)} all-gather(bf16[2,1,512]{2,0,1:T(2,128)(2,1)S(1)} %copy-done.10), channel_id=1, replica_groups=mesh['parts'=2,'turn'=4,'branch'=4] {'branch'}, dimensions={1}, use_global_device_ids=true | all-gather | bytes 10240 | tf_op jit(solution)/shard_map/all_gather | solution.py:126
  19.9 13.2 %all_gather.14 = bf16[2,8,512]{2,0,1:T(2,128)(2,1)S(1)} all-gather(bf16[2,2,512]{2,0,1:T(2,128)(2,1)S(1)} %copy.56), channel_id=1, replica_groups=mesh['parts'=2,'turn'=4,'branch'=4] {'branch'}, dimensions={1}, use_global_device_ids=true | all-gather | bytes 20480 | tf_op jit(solution)/shard_map/all_gather | solution.py:127
  33.3 5.2 %all_gather.13 = bf16[2,16,512]{2,0,1:T(2,128)(2,1)S(1)} all-gather(bf16[2,4,512]{2,0,1:T(2,128)(2,1)S(1)} %all_gather.12), channel_id=1, replica_groups=mesh['parts'=2,'turn'=4,'branch'=4] {'turn'}, dimensions={1}, use_global_device_ids=true | all-gather | bytes 40960 | tf_op jit(solution)/shard_map/all_gather | solution.py:130
  38.6 5.2 %all_gather.15 = bf16[2,32,512]{2,1,0:T(8,128)(2,1)S(1)} all-gather(bf16[2,8,512]{2,1,0:T(8,128)(2,1)S(1)} %copy.57), channel_id=1, replica_groups=mesh['parts'=2,'turn'=4,'branch'=4] {'turn'}, dimensions={1}, use_global_device_ids=true | all-gather | bytes 81920 | tf_op jit(solution)/shard_map/all_gather | solution.py:131
  43.9 0.8 broadcast.77.clone
  44.6 0.8 broadcast.77
  45.6 43.4 %while.30 = (s32[]{:T(128)}, bf16[128,4096]{1,0:T(8,128)(2,1)S(1)}, bf16[128,4096]{1,0:T(8,128)(2,1)S(1)}, f32[176,512]{1,0:T(8,128)}, f32[176,512]{1,0:T(8,128)...) while((s32[]{:T(128)}, bf16[128,4096]{1,0:T(8,128)(2,1)S(1)}, ...), condition=%wide.region_11.12_spmd, body=%wide.region_7.11_spmd.sunk | while | flops 373284352 | bytes 12505477 | solution.py:120
  45.7 1.1 constant_dynamic-slice_fusion.4
  46.9 1.0 constant_dynamic-slice_fusion.5
  48.1 1.2 fusion.100
  49.9 1.4 fusion.101
  51.4 2.0 %fusion.104 = f32[176,512]{1,0:T(8,128)} fusion(f32[176,512]{1,0:T(8,128)} %get-tuple-element.449, s32[]{:T(128)S(6)} %select_n.65, bf16[128,8,128]{0,2,1:T(8,128)(2,1)S(1)} %bitcast.177, f32[8,128]{1,0:T(8,128)S(1)} %get-tuple-element.408, bf16[128,8,128]{0,2,1:T(8,128)(2,1)S(1)} %bitcast.173, pred[128,176]{0,1:T(8,128)(4,1)S(1)} %get-tuple-element.467, ...), kind=kOutput, calls=%fused_computation.15.clone.1 | convolution fusion | flops 93177008 | bytes 687104 | tf_op jit(solution)/shard_map/while/body/eval_jaxpr/grk,rgd->kd/dot_general | solution.py:81
  53.4 0.9 fusion.103
  54.3 1.0 fusion.102
  55.6 0.8 copy-done.5
  56.5 1.1 constant_dynamic-slice_fusion.4
  57.8 1.0 constant_dynamic-slice_fusion.5
  58.9 1.2 fusion.100
  60.7 1.4 fusion.101
  62.3 2.0 %fusion.104 = f32[176,512]{1,0:T(8,128)} fusion(f32[176,512]{1,0:T(8,128)} %get-tuple-element.449, s32[]{:T(128)S(6)} %select_n.65, bf16[128,8,128]{0,2,1:T(8,128)(2,1)S(1)} %bitcast.177, f32[8,128]{1,0:T(8,128)S(1)} %get-tuple-element.408, bf16[128,8,128]{0,2,1:T(8,128)(2,1)S(1)} %bitcast.173, pred[128,176]{0,1:T(8,128)(4,1)S(1)} %get-tuple-element.467, ...), kind=kOutput, calls=%fused_computation.15.clone.1 | convolution fusion | flops 93177008 | bytes 687104 | tf_op jit(solution)/shard_map/while/body/eval_jaxpr/grk,rgd->kd/dot_general | solution.py:81
  64.2 0.9 fusion.103
  65.1 1.0 fusion.102
  66.4 0.8 copy-done.5
  67.3 1.1 constant_dynamic-slice_fusion.4
  68.6 1.0 constant_dynamic-slice_fusion.5
  69.8 1.2 fusion.100
  71.5 1.4 fusion.101
  73.1 2.0 %fusion.104 = f32[176,512]{1,0:T(8,128)} fusion(f32[176,512]{1,0:T(8,128)} %get-tuple-element.449, s32[]{:T(128)S(6)} %select_n.65, bf16[128,8,128]{0,2,1:T(8,128)(2,1)S(1)} %bitcast.177, f32[8,128]{1,0:T(8,128)S(1)} %get-tuple-element.408, bf16[128,8,128]{0,2,1:T(8,128)(2,1)S(1)} %bitcast.173, pred[128,176]{0,1:T(8,128)(4,1)S(1)} %get-tuple-element.467, ...), kind=kOutput, calls=%fused_computation.15.clone.1 | convolution fusion | flops 93177008 | bytes 687104 | tf_op jit(solution)/shard_map/while/body/eval_jaxpr/grk,rgd->kd/dot_general | solution.py:81
  75.1 0.9 fusion.103
  76.0 1.0 fusion.102
  77.2 0.8 copy-done.5
  78.2 1.1 constant_dynamic-slice_fusion.4
  79.4 1.0 constant_dynamic-slice_fusion.5
  80.6 1.2 fusion.100
  82.4 1.4 fusion.101
  83.9 2.0 %fusion.104 = f32[176,512]{1,0:T(8,128)} fusion(f32[176,512]{1,0:T(8,128)} %get-tuple-element.449, s32[]{:T(128)S(6)} %select_n.65, bf16[128,8,128]{0,2,1:T(8,128)(2,1)S(1)} %bitcast.177, f32[8,128]{1,0:T(8,128)S(1)} %get-tuple-element.408, bf16[128,8,128]{0,2,1:T(8,128)(2,1)S(1)} %bitcast.173, pred[128,176]{0,1:T(8,128)(4,1)S(1)} %get-tuple-element.467, ...), kind=kOutput, calls=%fused_computation.15.clone.1 | convolution fusion | flops 93177008 | bytes 687104 | tf_op jit(solution)/shard_map/while/body/eval_jaxpr/grk,rgd->kd/dot_general | solution.py:81
  85.9 0.9 fusion.103
  86.8 1.0 fusion.102
  88.0 0.8 copy-done.5
  89.0 0.9 slice_bitcast_fusion.6
  89.8 0.8 slice_bitcast_fusion.7
  90.9 0.7 pad_maximum_fusion
  91.6 63.5 %all-reduce.4 = (bf16[2,32,512]{2,1,0:T(8,128)(2,1)S(1)}, bf16[2,16,512]{2,0,1:T(2,128)(2,1)S(1)}) all-reduce(f32[2,32,512]{2,1,0:T(8,128)S(1)} %pad_maximum_fusion.3, f32[2,16,512]{2,0,1:T(2,128)S(1)} %copy.61), channel_id=2, replica_groups=mesh['parts'=2,'turn'=4,'branch'=4] {'turn','branch'}, use_global_device_ids=true, to_apply=%region_12.13.clone | all-reduce | flops 49152 | bytes 294912
  155.8 1.2 dynamic-slice_convert_fusion.1
  (111 shorter events, 9.5 us)
Async XLA Ops:
  0.6 0.7 copy-start.13
  2.6 0.7 copy-start.11
  3.5 0.7 copy-start.12
  4.9 0.7 copy-start.9
  5.6 0.7 copy-start.10
  33.2 10.6 %copy-start.6 = (bf16[2,128,512]{2,1,0:T(8,128)(2,1)S(1)}, bf16[2,128,512]{2,1,0:T(8,128)(2,1)}, u32[]{:S(2)}) copy-start(bf16[2,128,512]{2,1,0:T(8,128)(2,1)} %param.12) | copy-start | bytes 786436
  45.6 3.7 %copy-start.4 = (bf16[176,512]{1,0:T(8,128)(2,1)}, bf16[176,512]{1,0:T(8,128)(2,1)S(1)}, u32[]{:S(2)}) copy-start(bf16[176,512]{1,0:T(8,128)(2,1)S(1)} %get-tuple-element.468) | copy-start | bytes 540676 | tf_op jit(solution)/shard_map/while
  45.6 3.7 %copy-start.7 = (bf16[176,512]{1,0:T(8,128)(2,1)}, bf16[176,512]{1,0:T(8,128)(2,1)S(1)}, u32[]{:S(2)}) copy-start(bf16[176,512]{1,0:T(8,128)(2,1)S(1)} %get-tuple-element.466) | copy-start | bytes 540676 | tf_op jit(solution)/shard_map/while
  55.5 0.9 copy-start.5
  55.5 1.0 copy-start.8
  56.5 3.7 %copy-start.4 = (bf16[176,512]{1,0:T(8,128)(2,1)}, bf16[176,512]{1,0:T(8,128)(2,1)S(1)}, u32[]{:S(2)}) copy-start(bf16[176,512]{1,0:T(8,128)(2,1)S(1)} %get-tuple-element.468) | copy-start | bytes 540676 | tf_op jit(solution)/shard_map/while
  56.5 3.7 %copy-start.7 = (bf16[176,512]{1,0:T(8,128)(2,1)}, bf16[176,512]{1,0:T(8,128)(2,1)S(1)}, u32[]{:S(2)}) copy-start(bf16[176,512]{1,0:T(8,128)(2,1)S(1)} %get-tuple-element.466) | copy-start | bytes 540676 | tf_op jit(solution)/shard_map/while
  66.3 0.9 copy-start.5
  66.3 1.0 copy-start.8
  67.3 3.7 %copy-start.4 = (bf16[176,512]{1,0:T(8,128)(2,1)}, bf16[176,512]{1,0:T(8,128)(2,1)S(1)}, u32[]{:S(2)}) copy-start(bf16[176,512]{1,0:T(8,128)(2,1)S(1)} %get-tuple-element.468) | copy-start | bytes 540676 | tf_op jit(solution)/shard_map/while
  67.3 3.7 %copy-start.7 = (bf16[176,512]{1,0:T(8,128)(2,1)}, bf16[176,512]{1,0:T(8,128)(2,1)S(1)}, u32[]{:S(2)}) copy-start(bf16[176,512]{1,0:T(8,128)(2,1)S(1)} %get-tuple-element.466) | copy-start | bytes 540676 | tf_op jit(solution)/shard_map/while
  77.1 0.9 copy-start.5
  77.2 1.0 copy-start.8
  78.2 3.7 %copy-start.4 = (bf16[176,512]{1,0:T(8,128)(2,1)}, bf16[176,512]{1,0:T(8,128)(2,1)S(1)}, u32[]{:S(2)}) copy-start(bf16[176,512]{1,0:T(8,128)(2,1)S(1)} %get-tuple-element.468) | copy-start | bytes 540676 | tf_op jit(solution)/shard_map/while
  78.2 3.7 %copy-start.7 = (bf16[176,512]{1,0:T(8,128)(2,1)}, bf16[176,512]{1,0:T(8,128)(2,1)S(1)}, u32[]{:S(2)}) copy-start(bf16[176,512]{1,0:T(8,128)(2,1)S(1)} %get-tuple-element.466) | copy-start | bytes 540676 | tf_op jit(solution)/shard_map/while
  88.0 0.9 copy-start.5
  88.0 1.0 copy-start.8
  89.0 66.2 %copy-start = (bf16[128,4096]{1,0:T(8,128)(2,1)}, bf16[128,4096]{1,0:T(8,128)(2,1)S(1)}, u32[]{:S(2)}) copy-start(bf16[128,4096]{1,0:T(8,128)(2,1)S(1)} %get-tuple-element.279) | copy-start | bytes 3145732
  89.0 66.2 %copy-start.1 = (bf16[128,4096]{1,0:T(8,128)(2,1)}, bf16[128,4096]{1,0:T(8,128)(2,1)S(1)}, u32[]{:S(2)}) copy-start(bf16[128,4096]{1,0:T(8,128)(2,1)S(1)} %get-tuple-element.278) | copy-start | bytes 3145732
  89.0 1.8 %copy-start.2 = (f32[176,512]{1,0:T(8,128)S(1)}, f32[176,512]{1,0:T(8,128)}, u32[]{:S(2)}) copy-start(f32[176,512]{1,0:T(8,128)} %get-tuple-element.198) | copy-start | bytes 1081348
  89.8 1.0 copy-start.3
where the time goes:
time: 158 us; the launch traced here: 157 us
  blocking collectives  101 us (64%)
  matrix products  28.2 us (18%)
  local copies, waits for them, and re-layouts  23.9 us (15%)
  other arithmetic  2.21 us (1%)
    unnamed x1, blocking collectives  63.5 us
    all_gather x1, blocking collectives, on_device(): lax.all_gather(kv_trunk, 'branch', axis=1, tiled=True)  13.6 us
    all_gather x1, blocking collectives, on_device(): lax.all_gather(turn_key_value, 'branch', axis=1, tiled=True)  13.2 us
    dot_general x4, matrix products, group_terms(): jnp.einsum('grk,rgd->kd', rounded, cotangent, preferred_element_type=jnp....  7.87 us
    dot_general x4, matrix products, group_terms(): jnp.einsum('rgd,kd->grk', cotangent, head_values, preferred_element_type=...  5.57 us
    all_gather x1, blocking collectives, on_device(): lax.all_gather(nearby[1], 'turn', axis=1, tiled=True)  5.24 us
    all_gather x1, blocking collectives, on_device(): lax.all_gather(nearby[0], 'turn', axis=1, tiled=True)  5.19 us
    dynamic_slice x8, local copies, waits for them, and re-layouts, group_terms(): lax.dynamic_slice_in_dim(grad_out, start, group_width, 1)  5.05 us

commit v1 on v0

v1 whole, which is shorter than its diff:
```python
import functools
import math

import jax
import jax.numpy as jnp
from jax import lax
from jax.experimental import pallas as pl
from jax.experimental.pallas import tpu as pltpu
from jax.sharding import PartitionSpec as P

KEY_VALUE_HEADS = 4
HEAD_SIZE = 128
QUERY_PER_KEY = 8

masked_score = -1e30
MESH = pl.DeviceIdType.MESH
F32 = jnp.float32
BF16 = jnp.bfloat16


def dot(a, b, ca, cb):
    return lax.dot_general(a, b, (((ca,), (cb,)), ((), ())), preferred_element_type=F32)


def one_hot(cond):
    return jnp.where(cond, 1.0, 0.0).astype(BF16)


def kernel(
    turn_count, branch_count,
    query, bkv, turn_kv, trunk_kv, grad_out, lengths, parents,
    attended, grad_query, grad_branch, grad_turn, grad_trunk,
    q_v, do_v, kv_v, turn_v, trunk_v,
    pack32, pack, gathered, send, received,
    e_s, dp_s, m_s, l_s, c_s, f_s, d_s, psh_s, dssh_s, bias_s,
    ksh_s, vsh_s, o_v, dq_v, gkv_v,
    q_sem, do_sem, in_sem, own_sem, o_sem, dq_sem, gkv_sem,
    gsend_sem, grecv_sem, rsend_sem, rrecv_sem,
):
    n = turn_count * branch_count
    rows = query.shape[0]
    width = QUERY_PER_KEY * HEAD_SIZE
    pair = 2 * HEAD_SIZE
    pair_rows = 2 * rows
    pairs = QUERY_PER_KEY // 2
    trunk_own = trunk_kv.shape[1]
    turn_own = turn_kv.shape[1]
    own = trunk_own + turn_own
    trunk_rows = n * trunk_own
    turn_rows = n * turn_own
    shared = trunk_rows + turn_rows
    slot = pack.shape[0]
    half = pack.shape[1]
    scale = 1.0 / math.sqrt(HEAD_SIZE)
    log_scale = scale * math.log2(math.e)
    my_turn = lax.axis_index("turn")
    me = my_turn * branch_count + lax.axis_index("branch")

    def device(k):
        peer = lax.rem(me + k, n)
        return {"turn": lax.div(peer, branch_count), "branch": lax.rem(peer, branch_count)}

    barrier = pltpu.get_barrier_semaphore()

    def greet(k, carry):
        pl.semaphore_signal(barrier, inc=1, device_id=device(k), device_id_type=MESH)
        return carry

    lax.fori_loop(1, n, greet, 0)

    small = [
        pltpu.make_async_copy(trunk_kv, trunk_v, in_sem.at[0]),
        pltpu.make_async_copy(turn_kv, turn_v, in_sem.at[1]),
    ]
    kv_copy = pltpu.make_async_copy(bkv, kv_v, in_sem.at[2])
    for c in small:
        c.start()
    kv_copy.start()
    q_copies, do_copies = [], []
    for g in range(KEY_VALUE_HEADS):
        cols = pl.ds(g * width, width)
        q_copies.append(pltpu.make_async_copy(query.at[:, cols], q_v.at[:, cols], q_sem.at[g]))
        do_copies.append(
            pltpu.make_async_copy(grad_out.at[:, cols], do_v.at[:, cols], do_sem.at[g])
        )
        q_copies[g].start()
        do_copies[g].start()

    key_pos = lax.broadcasted_iota(jnp.int32, (rows, rows), 0)
    query_pos = lax.broadcasted_iota(jnp.int32, (rows, rows), 1)
    key_segment = jnp.zeros((rows, rows), jnp.int32)
    query_segment = jnp.zeros((rows, rows), jnp.int32)
    end = jnp.int32(0)
    for k in range(lengths.shape[1]):
        end = end + lengths[0, k]
        key_segment += jnp.where(key_pos >= end, 1, 0)
        query_segment += jnp.where(query_pos >= end, 1, 0)
    inside = (key_segment == query_segment) & (key_pos <= query_pos)
    bias_s[...] = jnp.where(inside, 0.0, masked_score)

    for c in small:
        c.wait()
    pack32[...] = jnp.zeros_like(pack32)
    for kv in range(2):
        trunk_piece = trunk_v[kv].astype(F32)
        turn_piece = turn_v[kv].astype(F32)
        for side in range(2):
            base = (kv * 2 + side) * own
            cols = slice(side * half, (side + 1) * half)
            pack32[base : base + trunk_own, :] = trunk_piece[:, cols]
            pack32[base + trunk_own : base + own, :] = turn_piece[:, cols]
    pack[...] = pack32[...].astype(BF16)

    def two(ref, g, p):
        first = g * width + p * pair
        return jnp.concatenate(
            [ref[:, first : first + HEAD_SIZE], ref[:, first + HEAD_SIZE : first + pair]], axis=0
        )

    bias2 = jnp.concatenate([bias_s[...], bias_s[...]], axis=1)

    def own_part(g):
        q_copies[g].wait()
        do_copies[g].wait()
        keys = kv_v[0, :, g * HEAD_SIZE : (g + 1) * HEAD_SIZE]
        values = kv_v[1, :, g * HEAD_SIZE : (g + 1) * HEAD_SIZE]
        for p in range(pairs):
            at = slice((g * pairs + p) * pair_rows, (g * pairs + p + 1) * pair_rows)
            scores = dot(keys, two(q_v, g, p), 1, 1) * log_scale + bias2
            largest = jnp.max(scores, axis=0, keepdims=True)
            e = jnp.exp2(scores - largest)
            dprob = dot(values, two(do_v, g, p), 1, 1)
            e_s[:, at] = e
            dp_s[:, at] = dprob
            m_s[:, at] = largest
            l_s[:, at] = jnp.sum(e, axis=0, keepdims=True)
            c_s[:, at] = jnp.sum(e * dprob, axis=0, keepdims=True)

    kv_copy.wait()

    pl.semaphore_wait(barrier, n - 1)
    mine = pl.ds(pl.multiple_of(me * slot, slot), slot)

    def give(k, carry):
        pltpu.make_async_remote_copy(
            src_ref=pack,
            dst_ref=gathered.at[mine],
            send_sem=gsend_sem,
            recv_sem=grecv_sem,
            device_id=device(k),
            device_id_type=MESH,
        ).start()
        return carry

    lax.fori_loop(1, n, give, 0)
    keep = pltpu.make_async_copy(pack, gathered.at[mine], own_sem.at[0])
    keep.start()

    for g in range(KEY_VALUE_HEADS):
        own_part(g)

    keep.wait()
    others = pl.ds(0, (n - 1) * slot)
    all_in = pltpu.make_async_remote_copy(
        src_ref=gathered.at[others],
        dst_ref=gathered.at[others],
        send_sem=gsend_sem,
        recv_sem=grecv_sem,
        device_id=device(1),
        device_id_type=MESH,
    )
    all_in.wait_recv()

    def place(shape, row_axis):
        row = lax.broadcasted_iota(jnp.int32, shape, row_axis)
        is_trunk = row < trunk_rows
        late = row - trunk_rows
        owner = jnp.where(is_trunk, row // trunk_own, late // turn_own)
        inner = jnp.where(is_trunk, row % trunk_own, late % turn_own + trunk_own)
        return owner * slot + inner

    source = place((shared, n * slot), 0)
    column = lax.broadcasted_iota(jnp.int32, (shared, n * slot), 1)
    for kv, ref in ((0, ksh_s), (1, vsh_s)):
        for side in range(2):
            pick = one_hot(column == source + (kv * 2 + side) * own)
            ref[:, side * half : (side + 1) * half] = dot(pick, gathered[...], 1, 0).astype(BF16)

    row = lax.broadcasted_iota(jnp.int32, (shared, pair_rows), 0)
    owner_turn = lax.div(row - trunk_rows, turn_rows // turn_count)
    on_path = row < trunk_rows
    current = my_turn
    for step in range(turn_count):
        on_path = on_path | ((row >= trunk_rows) & (owner_turn == current))
        parent = parents[jnp.maximum(current, 0)]
        current = jnp.where(current >= 0, parent, -1)
    shared_bias = jnp.where(on_path, 0.0, masked_score)

    key_parts, value_parts = [], []
    for g in range(KEY_VALUE_HEADS):
        head = slice(g * HEAD_SIZE, (g + 1) * HEAD_SIZE)
        keys = ksh_s[:, head]
        values = vsh_s[:, head]
        grad_keys = jnp.zeros((shared, HEAD_SIZE), F32)
        grad_values = jnp.zeros((shared, HEAD_SIZE), F32)
        for p in range(pairs):
            at = slice((g * pairs + p) * pair_rows, (g * pairs + p + 1) * pair_rows)
            queries = two(q_v, g, p)
            cotangent = two(do_v, g, p)
            scores = dot(keys, queries, 1, 1) * log_scale + shared_bias
            dprob = dot(values, cotangent, 1, 1)
            m_own = m_s[:, at]
            largest = jnp.maximum(m_own, jnp.max(scores, axis=0, keepdims=True))
            e = jnp.exp2(scores - largest)
            factor = jnp.exp2(m_own - largest)
            inverse = 1.0 / (l_s[:, at] * factor + jnp.sum(e, axis=0, keepdims=True))
            delta = (c_s[:, at] * factor + jnp.sum(e * dprob, axis=0, keepdims=True)) * inverse
            probs = e * inverse
            weights = probs.astype(BF16)
            dscore = (probs * (dprob - delta)).astype(BF16)
            f_s[:, at] = factor * inverse
            d_s[:, at] = delta
            psh_s[:, at] = weights
            dssh_s[:, at] = dscore
            grad_keys += dot(dscore, queries, 1, 0)
            grad_values += dot(weights, cotangent, 1, 0)
        key_parts.append((grad_keys * scale).astype(BF16))
        value_parts.append(grad_values.astype(BF16))

    target = place((n * slot, shared), 1)
    line = lax.broadcasted_iota(jnp.int32, (n * slot, shared), 0)
    total = jnp.zeros((n * slot, half), F32)
    per_side = KEY_VALUE_HEADS // 2
    for kv, parts in ((0, key_parts), (1, value_parts)):
        for side in range(2):
            put = one_hot(line == target + (kv * 2 + side) * own)
            piece = jnp.concatenate(parts[side * per_side : (side + 1) * per_side], axis=1)
            total += dot(put, piece, 1, 0)
    send[...] = total.astype(BF16)

    def give_back(k, carry):
        peer = lax.rem(me + k, n)
        pltpu.make_async_remote_copy(
            src_ref=send.at[pl.ds(pl.multiple_of(peer * slot, slot), slot)],
            dst_ref=received.at[mine],
            send_sem=rsend_sem,
            recv_sem=rrecv_sem,
            device_id=device(k),
            device_id_type=MESH,
        ).start()
        return carry

    lax.fori_loop(1, n, give_back, 0)
    keep = pltpu.make_async_copy(send.at[mine], received.at[mine], own_sem.at[1])
    keep.start()

    outs = []
    for g in range(KEY_VALUE_HEADS):
        head = slice(g * HEAD_SIZE, (g + 1) * HEAD_SIZE)
        keys = jnp.concatenate([kv_v[0, :, head], ksh_s[:, head]], axis=0)
        values = jnp.concatenate([kv_v[1, :, head], vsh_s[:, head]], axis=0)
        grad_keys = jnp.zeros((rows, HEAD_SIZE), F32)
        grad_values = jnp.zeros((rows, HEAD_SIZE), F32)
        for p in range(pairs):
            at = slice((g * pairs + p) * pair_rows, (g * pairs + p + 1) * pair_rows)
            probs = e_s[:, at] * f_s[:, at]
            weights = probs.astype(BF16)
            dscore = (probs * (dp_s[:, at] - d_s[:, at])).astype(BF16)
            grad_keys += dot(dscore, two(q_v, g, p), 1, 0)
            grad_values += dot(weights, two(do_v, g, p), 1, 0)
            all_weights = jnp.concatenate([weights, psh_s[:, at]], axis=0)
            all_dscore = jnp.concatenate([dscore, dssh_s[:, at]], axis=0)
            out = dot(all_weights, values, 0, 0).astype(BF16)
            out_q = (dot(all_dscore, keys, 0, 0) * scale).astype(BF16)
            first = g * width + p * pair
            for i in range(2):
                cols = slice(first + i * HEAD_SIZE, first + (i + 1) * HEAD_SIZE)
                o_v[:, cols] = out[i * rows : (i + 1) * rows]
                dq_v[:, cols] = out_q[i * rows : (i + 1) * rows]
        gkv_v[0, :, head] = (grad_keys * scale).astype(BF16)
        gkv_v[1, :, head] = grad_values.astype(BF16)
        cols = pl.ds(g * width, width)
        outs.append(pltpu.make_async_copy(o_v.at[:, cols], attended.at[:, cols], o_sem.at[g]))
        outs.append(pltpu.make_async_copy(dq_v.at[:, cols], grad_query.at[:, cols], dq_sem.at[g]))
        outs[-2].start()
        outs[-1].start()
    outs.append(pltpu.make_async_copy(gkv_v, grad_branch, gkv_sem))
    outs[-1].start()

    keep.wait()
    back_in = pltpu.make_async_remote_copy(
        src_ref=received.at[others],
        dst_ref=received.at[others],
        send_sem=rsend_sem,
        recv_sem=rrecv_sem,
        device_id=device(1),
        device_id_type=MESH,
    )
    back_in.wait_recv()
    summed = jnp.zeros((slot, half), F32)
    for d in range(n):
        summed += received[d * slot : (d + 1) * slot, :].astype(F32)
    pack32[...] = summed
    for kv in range(2):
        for side in range(2):
            base = (kv * 2 + side) * own
            cols = slice(side * half, (side + 1) * half)
            grad_trunk[kv, :, cols] = pack32[base : base + trunk_own, :].astype(BF16)
            grad_turn[kv, :, cols] = pack32[base + trunk_own : base + own, :].astype(BF16)
    all_in.wait_send()
    back_in.wait_send()
    for c in outs:
        c.wait()


def on_device(query, branch_key_value, turn_key_value, kv_trunk, grad_out, branch_lengths, parents):
    turn_count = lax.axis_size("turn")
    branch_count = lax.axis_size("branch")
    n = turn_count * branch_count
    rows, features = query.shape
    kv_width = branch_key_value.shape[2]
    own = kv_trunk.shape[1] + turn_key_value.shape[1]
    shared = n * own
    slot = -(-4 * own // 16) * 16
    half = kv_width // 2
    total = rows * (features // HEAD_SIZE)
    anywhere = pl.BlockSpec(memory_space=pl.ANY)
    scalar = pl.BlockSpec(memory_space=pltpu.SMEM)
    vector = pl.BlockSpec(memory_space=pltpu.VMEM)
    dma = pltpu.SemaphoreType.DMA
    like = lambda a: jax.ShapeDtypeStruct(a.shape, a.dtype)
    return pl.pallas_call(
        functools.partial(kernel, turn_count, branch_count),
        out_shape=(
            like(query), like(query), like(branch_key_value), like(turn_key_value), like(kv_trunk)
        ),
        in_specs=[anywhere] * 5 + [scalar, scalar],
        out_specs=(anywhere, anywhere, anywhere, vector, vector),
        scratch_shapes=[
            pltpu.VMEM(query.shape, BF16),
            pltpu.VMEM(query.shape, BF16),
            pltpu.VMEM(branch_key_value.shape, BF16),
            pltpu.VMEM(turn_key_value.shape, BF16),
            pltpu.VMEM(kv_trunk.shape, BF16),
            pltpu.VMEM((slot, half), F32),
            pltpu.VMEM((slot, half), BF16),
            pltpu.VMEM((n * slot, half), BF16),
            pltpu.VMEM((n * slot, half), BF16),
            pltpu.VMEM((n * slot, half), BF16),
            pltpu.VMEM((rows, total), F32),
            pltpu.VMEM((rows, total), F32),
            pltpu.VMEM((1, total), F32),
            pltpu.VMEM((1, total), F32),
            pltpu.VMEM((1, total), F32),
            pltpu.VMEM((1, total), F32),
            pltpu.VMEM((1, total), F32),
            pltpu.VMEM((shared, total), BF16),
            pltpu.VMEM((shared, total), BF16),
            pltpu.VMEM((rows, rows), F32),
            pltpu.VMEM((shared, kv_width), BF16),
            pltpu.VMEM((shared, kv_width), BF16),
            pltpu.VMEM(query.shape, BF16),
            pltpu.VMEM(query.shape, BF16),
            pltpu.VMEM(branch_key_value.shape, BF16),
            dma((KEY_VALUE_HEADS,)),
            dma((KEY_VALUE_HEADS,)),
            dma((3,)),
            dma((2,)),
            dma((KEY_VALUE_HEADS,)),
            dma((KEY_VALUE_HEADS,)),
            dma,
            dma,
            dma,
            dma,
            dma,
        ],
        compiler_params=pltpu.CompilerParams(collective_id=0, has_side_effects=True),
    )(query, branch_key_value, turn_key_value, kv_trunk, grad_out, branch_lengths, parents)


def solution(mesh):
    every = ("parts", "turn", "branch")
    row = P(every, None)
    middle = P(None, every, None)
    return jax.shard_map(
        on_device,
        mesh=mesh,
        in_specs=(row, middle, middle, middle, row, row, P("parts")),
        out_specs=(row, row, middle, middle, middle),
        check_vma=False,
    )
```

time: 158 us -> 29.3 us (0.19)
  blocking collectives: 101 us -> 0 us
  matrix products: 28.2 us -> 0 us
  Pallas kernels: 0 us -> 21.1 us
  local copies, waits for them, and re-layouts: 23.9 us -> 7.29 us
  other arithmetic: 2.21 us -> 0 us
    unnamed x1 -> x0, blocking collectives: 63.5 us -> none
    all_gather x4 -> x0, blocking collectives: 37.3 us -> none  [the longest x1 13.6 us: on_device(): lax.all_gather(kv_trunk, 'branch', axis=1, tiled=True)]
    dot_general x20 -> x0, matrix products: 23.3 us -> none  [the longest x4 7.87 us: group_terms(): jnp.einsum('grk,rgd->kd', rounded, cotangent, preferred_element_type=jnp....]
    pallas_call x0 -> x1, Pallas kernels: none -> 21.1 us  [on_device(): pl.pallas_call(functools.partial(kernel, turn_count, branch_count), out_s...]
    dynamic_slice x16 -> x0, local copies, waits for them, and re-layouts: 9.62 us -> none  [the longest x8 5.05 us: group_terms(): lax.dynamic_slice_in_dim(grad_out, start, group_width, 1)]
    sub x4 -> x0, matrix products: 4.87 us -> none  [group_terms(): exponent = jnp.exp(scores - largest)]
    while x32 -> x0, local copies, waits for them, and re-layouts: 3.79 us -> none
    another operation x11 -> x0, local copies, waits for them, and re-layouts: 3.52 us -> none  [the longest x3 1.74 us: on_device(): grad_trunk = jnp.stack([grad_keys[:trunk_rows], grad_values[:trunk_rows]])]
where the time goes in v1:
time: 29.3 us; the launch traced here: 29.1 us
  Pallas kernels  21.1 us (72%)
  local copies, waits for them, and re-layouts  7.29 us (25%)
  between operations  0.65 us (2%)
    pallas_call x1, Pallas kernels, on_device(): pl.pallas_call(functools.partial(kernel, turn_count, branch_count), out_s...  21.1 us
    unnamed x13, local copies, waits for them, and re-layouts  6.71 us

profile of v1, /device:TPU:0, one launch (start us, length us, event | category | flops | bytes accessed | tf_op | source)
XLA Modules:
  0.0 29.1 jit_solution(2700916535187215003)
XLA Ops:
  0.6 1.3 %copy.12.trunk_kv = bf16[2,1,512]{2,1,0:T(2,128)(2,1)} copy(bf16[2,1,512]{2,0,1:T(2,128)(2,1)} %param.10) | data formatting | bytes 4096 | tf_op args[3]
  1.9 21.1 %shard_map.110 = (bf16[128,4096]{1,0:T(8,128)(2,1)}, bf16[128,4096]{1,0:T(8,128)(2,1)}, bf16[2,128,512]{2,1,0:T(8,128)(2,1)}, bf16[2,2,512]{2,1,0:T(2,128)(2,1)}, bf16[2,1,512]{2,1,0:T(2,128)(2,1)}) custom-call(bf16[128,4096]{1,0:T(8,128)(2,1)} %query.1, bf16[2,128,512]{2,1,0:T(8,128)(2,1)} %bkv.1, bf16[2,2,512]{2,1,0:T(2,128)(2,1)} %turn_kv.1, ...), custom_call_target="tpu_custom_call" | custom-call | tf_op jit(solution)/shard_map/pallas_call | solution.py:332
  23.0 0.0 copy-start.2
  23.0 0.7 %copy-done.2 = bf16[2,1,512]{2,1,0:T(2,128)(2,1)S(1)} copy-done((bf16[2,1,512]{2,1,0:T(2,128)(2,1)S(1)}, bf16[2,1,512]{2,1,0:T(2,128)(2,1)}, u32[]{:S(2)}) %copy-start.2) | copy-done | bytes 2072
  23.7 0.6 %copy.13 = bf16[2,1,512]{2,0,1:T(2,128)(2,1)} copy(bf16[2,1,512]{2,1,0:T(2,128)(2,1)S(1)} %copy-done.2) | data formatting | bytes 4096 | tf_op jit(solution)/shard_map/pallas_call | solution.py:332
  24.3 0.0 copy-start
  24.3 2.4 %copy.18 = bf16[128,4096]{1,0:T(8,128)(2,1)} copy(bf16[128,4096]{1,0:T(8,128)(2,1)} %get-tuple-element.15) | data formatting | bytes 2097152
  26.7 0.0 copy-done
  26.7 0.0 copy-start.1
  26.7 1.0 %copy.19 = bf16[128,4096]{1,0:T(8,128)(2,1)} copy(bf16[128,4096]{1,0:T(8,128)(2,1)S(1)} %copy-done) | data formatting | bytes 2097152
  27.6 0.1 copy-done.1
  27.8 0.0 copy-start.3
  27.8 0.7 %copy.20 = bf16[2,128,512]{2,1,0:T(8,128)(2,1)} copy(bf16[2,128,512]{2,1,0:T(8,128)(2,1)S(1)} %copy-done.1) | data formatting | bytes 524288
  28.5 0.0 copy-done.3
  28.5 0.6 %copy.21 = bf16[2,2,512]{2,1,0:T(2,128)(2,1)} copy(bf16[2,2,512]{2,1,0:T(2,128)(2,1)S(1)} %copy-done.3) | data formatting | bytes 8192
Async XLA Ops:
  23.0 0.7 %copy-start.2 = (bf16[2,1,512]{2,1,0:T(2,128)(2,1)S(1)}, bf16[2,1,512]{2,1,0:T(2,128)(2,1)}, u32[]{:S(2)}) copy-start(bf16[2,1,512]{2,1,0:T(2,128)(2,1)} %get-tuple-element.9) | copy-start | bytes 6148
  24.3 2.4 %copy-start = (bf16[128,4096]{1,0:T(8,128)(2,1)S(1)}, bf16[128,4096]{1,0:T(8,128)(2,1)}, u32[]{:S(2)}) copy-start(bf16[128,4096]{1,0:T(8,128)(2,1)} %get-tuple-element.16) | copy-start | bytes 3145732
  26.7 1.1 %copy-start.1 = (bf16[2,128,512]{2,1,0:T(8,128)(2,1)S(1)}, bf16[2,128,512]{2,1,0:T(8,128)(2,1)}, u32[]{:S(2)}) copy-start(bf16[2,128,512]{2,1,0:T(8,128)(2,1)} %get-tuple-element.17) | copy-start | bytes 786436
  27.8 0.7 %copy-start.3 = (bf16[2,2,512]{2,1,0:T(2,128)(2,1)S(1)}, bf16[2,2,512]{2,1,0:T(2,128)(2,1)}, u32[]{:S(2)}) copy-start(bf16[2,2,512]{2,1,0:T(2,128)(2,1)} %get-tuple-element.18) | copy-start | bytes 12292

commit v2 on v1

v2 whole, which is shorter than its diff:
```python
import functools
import math

import jax
import jax.numpy as jnp
from jax import lax
from jax.experimental import pallas as pl
from jax.experimental.pallas import tpu as pltpu
from jax.sharding import PartitionSpec as P

KEY_VALUE_HEADS = 4
HEAD_SIZE = 128
QUERY_PER_KEY = 8

masked_score = -1e30
MESH = pl.DeviceIdType.MESH
F32 = jnp.float32
BF16 = jnp.bfloat16


def dot(a, b, ca, cb):
    return lax.dot_general(a, b, (((ca,), (cb,)), ((), ())), preferred_element_type=F32)


def one_hot(cond):
    return jnp.where(cond, 1.0, 0.0).astype(BF16)


def split(x, d):
    if d & (d - 1) == 0:
        return lax.shift_right_arithmetic(x, d.bit_length() - 1), x & (d - 1)
    return lax.div(x, d), lax.rem(x, d)


def kernel(
    turn_count, branch_count,
    query, bkv, turn_kv, trunk_kv, grad_out, lengths_in, parents_in,
    o_v, dq_v, gkv_v, grad_turn, grad_trunk,
    lengths, parents, q_v, do_v, kv_v, turn_v, trunk_v,
    pack32, pack, gathered, send, received, pick_s, put_s,
    e_s, dp_s, m_s, l_s, c_s, f_s, d_s, psh_s, dssh_s, bias_s, path_s,
    ksh_s, vsh_s,
    q_sem, do_sem, in_sem, own_sem,
    gsend_sem, grecv_sem, rsend_sem, rrecv_sem,
):
    n = turn_count * branch_count
    rows = query.shape[0]
    width = QUERY_PER_KEY * HEAD_SIZE
    pair = 2 * HEAD_SIZE
    pair_rows = 2 * rows
    pairs = QUERY_PER_KEY // 2
    trunk_own = trunk_kv.shape[0]
    turn_own = turn_kv.shape[1]
    own = trunk_own + turn_own
    trunk_rows = n * trunk_own
    turn_rows = n * turn_own
    shared = trunk_rows + turn_rows
    slot = pack.shape[1]
    sides = pack.shape[0]
    per_side = KEY_VALUE_HEADS // sides
    chunk = put_s.shape[1] // slot
    chunk_trunk, chunk_turn = chunk * trunk_own, chunk * turn_own
    scale = 1.0 / math.sqrt(HEAD_SIZE)
    log_scale = scale * math.log2(math.e)
    my_turn = lax.axis_index("turn")
    me = my_turn * branch_count + lax.axis_index("branch")

    def device(k):
        peer = lax.rem(me + k, n)
        return {"turn": lax.div(peer, branch_count), "branch": lax.rem(peer, branch_count)}

    barrier = pltpu.get_barrier_semaphore()

    def greet(k, carry):
        pl.semaphore_signal(barrier, inc=1, device_id=device(k), device_id_type=MESH)
        return carry

    lax.fori_loop(1, n, greet, 0)

    small = [
        pltpu.make_async_copy(trunk_kv, trunk_v, in_sem.at[0]),
        pltpu.make_async_copy(turn_kv, turn_v, in_sem.at[1]),
    ]
    scalars = [
        pltpu.make_async_copy(lengths_in, lengths, in_sem.at[3]),
        pltpu.make_async_copy(parents_in, parents, in_sem.at[4]),
    ]
    kv_copy = pltpu.make_async_copy(bkv, kv_v, in_sem.at[2])
    for c in small + scalars:
        c.start()
    kv_copy.start()
    q_copies, do_copies = [], []
    for g in range(KEY_VALUE_HEADS):
        cols = pl.ds(g * width, width)
        q_copies.append(pltpu.make_async_copy(query.at[:, cols], q_v.at[:, cols], q_sem.at[g]))
        do_copies.append(
            pltpu.make_async_copy(grad_out.at[:, cols], do_v.at[:, cols], do_sem.at[g])
        )
        q_copies[g].start()
        do_copies[g].start()

    for c in small:
        c.wait()
    pack32[...] = jnp.zeros_like(pack32)
    for kv in range(2):
        turn_piece = turn_v[kv].astype(F32)
        for g in range(KEY_VALUE_HEADS):
            base = (kv * per_side + g % per_side) * own
            cols = slice(g * HEAD_SIZE, (g + 1) * HEAD_SIZE)
            for r in range(trunk_own):
                pack32[g // per_side, base + r : base + r + 1, :] = trunk_v[r].astype(F32)[
                    kv : kv + 1, cols
                ]
            pack32[g // per_side, base + trunk_own : base + own, :] = turn_piece[:, cols]
    pack[...] = pack32[...].astype(BF16)

    def place(shape, axis):
        row = lax.broadcasted_iota(jnp.int32, shape, axis)
        trunk_owner, trunk_inner = split(row, trunk_own)
        turn_owner, turn_inner = split(row - chunk_trunk, turn_own)
        is_trunk = row < chunk_trunk
        owner = jnp.where(is_trunk, trunk_owner, turn_owner)
        return owner * slot + jnp.where(is_trunk, trunk_inner, turn_inner + trunk_own)

    chunk_shared = chunk * own
    source = place((chunk_shared, 1), 0)
    column = lax.broadcasted_iota(jnp.int32, (chunk_shared, chunk * slot), 1)
    target = place((1, chunk_shared), 1)
    line = lax.broadcasted_iota(jnp.int32, (chunk * slot, chunk_shared), 0)
    for b in range(2 * per_side):
        pick_s[b] = one_hot(column == source + b * own)
        put_s[b] = one_hot(line == target + b * own)

    def in_order(b, side):
        pieces = [
            dot(pick_s[b], gathered[side, c * chunk * slot : (c + 1) * chunk * slot], 1, 0)
            for c in range(n // chunk)
        ]
        if len(pieces) > 1:
            pieces = [x[:chunk_trunk] for x in pieces] + [x[chunk_trunk:] for x in pieces]
        return jnp.concatenate(pieces, axis=0).astype(BF16)

    def chunk_rows(x, c):
        if n == chunk:
            return x
        first = trunk_rows + c * chunk_turn
        return jnp.concatenate(
            [x[c * chunk_trunk : (c + 1) * chunk_trunk], x[first : first + chunk_turn]], axis=0
        )

    for c in scalars:
        c.wait()
    key_pos = lax.broadcasted_iota(jnp.int32, (rows, 1), 0)
    query_pos = lax.broadcasted_iota(jnp.int32, (1, rows), 1)
    key_segment = jnp.zeros((rows, 1), jnp.int32)
    query_segment = jnp.zeros((1, rows), jnp.int32)
    end = jnp.int32(0)
    for k in range(lengths.shape[1]):
        end = end + lengths[0, k]
        key_segment += jnp.where(key_pos >= end, 1, 0)
        query_segment += jnp.where(query_pos >= end, 1, 0)
    inside = (key_segment == query_segment) & (key_pos <= query_pos)
    bias_s[...] = jnp.where(inside, 0.0, masked_score)

    row = lax.broadcasted_iota(jnp.int32, (shared, HEAD_SIZE), 0)
    owner_turn, _ = split(row - trunk_rows, turn_rows // turn_count)
    on_path = row < trunk_rows
    current = my_turn
    for step in range(turn_count):
        on_path = on_path | ((row >= trunk_rows) & (owner_turn == current))
        parent = parents[jnp.maximum(current, 0)]
        current = jnp.where(current >= 0, parent, -1)
    path_s[...] = jnp.where(on_path, 0.0, masked_score)

    def two(ref, g, p):
        first = g * width + p * pair
        return jnp.concatenate(
            [ref[:, first : first + HEAD_SIZE], ref[:, first + HEAD_SIZE : first + pair]], axis=0
        )

    def own_part(g):
        q_copies[g].wait()
        do_copies[g].wait()
        keys = kv_v[0, :, g * HEAD_SIZE : (g + 1) * HEAD_SIZE]
        values = kv_v[1, :, g * HEAD_SIZE : (g + 1) * HEAD_SIZE]
        bias2 = jnp.concatenate([bias_s[...], bias_s[...]], axis=1)
        for p in range(pairs):
            at = slice((g * pairs + p) * pair_rows, (g * pairs + p + 1) * pair_rows)
            scores = dot(keys, two(q_v, g, p), 1, 1) * log_scale + bias2
            largest = jnp.max(scores, axis=0, keepdims=True)
            e = jnp.exp2(scores - largest)
            dprob = dot(values, two(do_v, g, p), 1, 1)
            e_s[:, at] = e
            dp_s[:, at] = dprob
            m_s[:, at] = largest
            l_s[:, at] = jnp.sum(e, axis=0, keepdims=True)
            c_s[:, at] = jnp.sum(e * dprob, axis=0, keepdims=True)

    pl.semaphore_wait(barrier, n - 1)
    mine = pl.ds(pl.multiple_of(me * slot, slot), slot)
    others = pl.ds(0, (n - 1) * slot)

    keeps, all_in = [], []
    for side in range(sides):

        def give(k, carry, side=side):
            pltpu.make_async_remote_copy(
                src_ref=pack.at[side],
                dst_ref=gathered.at[side, mine],
                send_sem=gsend_sem.at[side],
                recv_sem=grecv_sem.at[side],
                device_id=device(k),
                device_id_type=MESH,
            ).start()
            return carry

        lax.fori_loop(1, n, give, 0)
        keeps.append(
            pltpu.make_async_copy(pack.at[side], gathered.at[side, mine], own_sem.at[side])
        )
        keeps[side].start()
        all_in.append(
            pltpu.make_async_remote_copy(
                src_ref=gathered.at[side, others],
                dst_ref=gathered.at[side, others],
                send_sem=gsend_sem.at[side],
                recv_sem=grecv_sem.at[side],
                device_id=device(1),
                device_id_type=MESH,
            )
        )

    kv_copy.wait()
    for g in range(KEY_VALUE_HEADS):
        own_part(g)

    back_in, keeps_back = [], []
    for side in range(sides):
        keeps[side].wait()
        all_in[side].wait_recv()
        placed = [in_order(b, side) for b in range(2 * per_side)]
        for i in range(per_side):
            g = side * per_side + i
            head = slice(g * HEAD_SIZE, (g + 1) * HEAD_SIZE)
            ksh_s[:, head] = placed[i]
            vsh_s[:, head] = placed[per_side + i]

        shared_bias = jnp.concatenate([path_s[...]] * (pair_rows // HEAD_SIZE), axis=1)
        key_grads, value_grads = [], []
        for i in range(per_side):
            g = side * per_side + i
            keys = placed[i]
            values = placed[per_side + i]
            grad_keys = jnp.zeros((shared, HEAD_SIZE), F32)
            grad_values = jnp.zeros((shared, HEAD_SIZE), F32)
            for p in range(pairs):
                at = slice((g * pairs + p) * pair_rows, (g * pairs + p + 1) * pair_rows)
                queries = two(q_v, g, p)
                cotangent = two(do_v, g, p)
                scores = dot(keys, queries, 1, 1) * log_scale + shared_bias
                dprob = dot(values, cotangent, 1, 1)
                m_own = m_s[:, at]
                largest = jnp.maximum(m_own, jnp.max(scores, axis=0, keepdims=True))
                e = jnp.exp2(scores - largest)
                factor = jnp.exp2(m_own - largest)
                inverse = 1.0 / (l_s[:, at] * factor + jnp.sum(e, axis=0, keepdims=True))
                delta = (c_s[:, at] * factor + jnp.sum(e * dprob, axis=0, keepdims=True)) * inverse
                probs = e * inverse
                weights = probs.astype(BF16)
                dscore = (probs * (dprob - delta)).astype(BF16)
                f_s[:, at] = factor * inverse
                d_s[:, at] = delta
                psh_s[:, at] = weights
                dssh_s[:, at] = dscore
                grad_keys += dot(dscore, queries, 1, 0)
                grad_values += dot(weights, cotangent, 1, 0)
            key_grads.append((grad_keys * scale).astype(BF16))
            value_grads.append(grad_values.astype(BF16))
        for c in range(n // chunk):
            total = jnp.zeros((chunk * slot, HEAD_SIZE), F32)
            for b, x in enumerate(key_grads + value_grads):
                total += dot(put_s[b], chunk_rows(x, c), 1, 0)
            send[side, c * chunk * slot : (c + 1) * chunk * slot] = total.astype(BF16)

        def give_back(k, carry, side=side):
            peer = lax.rem(me + k, n)
            pltpu.make_async_remote_copy(
                src_ref=send.at[side, pl.ds(pl.multiple_of(peer * slot, slot), slot)],
                dst_ref=received.at[side, mine],
                send_sem=rsend_sem.at[side],
                recv_sem=rrecv_sem.at[side],
                device_id=device(k),
                device_id_type=MESH,
            ).start()
            return carry

        lax.fori_loop(1, n, give_back, 0)
        keeps_back.append(
            pltpu.make_async_copy(
                send.at[side, mine], received.at[side, mine], own_sem.at[sides + side]
            )
        )
        keeps_back[side].start()
        back_in.append(
            pltpu.make_async_remote_copy(
                src_ref=received.at[side, others],
                dst_ref=received.at[side, others],
                send_sem=rsend_sem.at[side],
                recv_sem=rrecv_sem.at[side],
                device_id=device(1),
                device_id_type=MESH,
            )
        )

    for g in range(KEY_VALUE_HEADS):
        head = slice(g * HEAD_SIZE, (g + 1) * HEAD_SIZE)
        keys = jnp.concatenate([kv_v[0, :, head], ksh_s[:, head]], axis=0)
        values = jnp.concatenate([kv_v[1, :, head], vsh_s[:, head]], axis=0)
        grad_keys = jnp.zeros((rows, HEAD_SIZE), F32)
        grad_values = jnp.zeros((rows, HEAD_SIZE), F32)
        for p in range(pairs):
            at = slice((g * pairs + p) * pair_rows, (g * pairs + p + 1) * pair_rows)
            probs = e_s[:, at] * f_s[:, at]
            weights = probs.astype(BF16)
            dscore = (probs * (dp_s[:, at] - d_s[:, at])).astype(BF16)
            grad_keys += dot(dscore, two(q_v, g, p), 1, 0)
            grad_values += dot(weights, two(do_v, g, p), 1, 0)
            all_weights = jnp.concatenate([weights, psh_s[:, at]], axis=0)
            all_dscore = jnp.concatenate([dscore, dssh_s[:, at]], axis=0)
            out = dot(all_weights, values, 0, 0).astype(BF16)
            out_q = (dot(all_dscore, keys, 0, 0) * scale).astype(BF16)
            first = g * width + p * pair
            for i in range(2):
                cols = slice(first + i * HEAD_SIZE, first + (i + 1) * HEAD_SIZE)
                o_v[:, cols] = out[i * rows : (i + 1) * rows]
                dq_v[:, cols] = out_q[i * rows : (i + 1) * rows]
        gkv_v[0, :, head] = (grad_keys * scale).astype(BF16)
        gkv_v[1, :, head] = grad_values.astype(BF16)

    for side in range(sides):
        keeps_back[side].wait()
        back_in[side].wait_recv()
        summed = jnp.zeros((slot, HEAD_SIZE), F32)
        for d in range(n):
            summed += received[side, d * slot : (d + 1) * slot, :].astype(F32)
        pack32[side] = summed
        for i in range(per_side):
            g = side * per_side + i
            cols = slice(g * HEAD_SIZE, (g + 1) * HEAD_SIZE)
            for kv in range(2):
                base = (kv * per_side + i) * own
                grad_turn[kv, :, cols] = pack32[side, base + trunk_own : base + own, :].astype(BF16)
            for r in range(trunk_own):
                key_at, value_at = i * own + r, (per_side + i) * own + r
                grad_trunk[r, :, cols] = jnp.concatenate(
                    [pack32[side, key_at : key_at + 1, :], pack32[side, value_at : value_at + 1, :]],
                    axis=0,
                ).astype(BF16)
    for side in range(sides):
        all_in[side].wait_send()
        back_in[side].wait_send()


def put_out(*refs):
    count = len(refs) // 2
    sems = refs[-1]
    copies = [
        pltpu.make_async_copy(refs[i], refs[count + i], sems.at[i]) for i in range(count)
    ]
    for c in copies:
        c.start()
    for c in copies:
        c.wait()


def on_device(query, branch_key_value, turn_key_value, kv_trunk, grad_out, branch_lengths, parents):
    turn_count = lax.axis_size("turn")
    branch_count = lax.axis_size("branch")
    n = turn_count * branch_count
    rows, features = query.shape
    kv_width = branch_key_value.shape[2]
    trunk = jnp.transpose(kv_trunk, (1, 0, 2))
    own = trunk.shape[0] + turn_key_value.shape[1]
    shared = n * own
    sides = 2
    per_side = KEY_VALUE_HEADS // sides
    slot = -(-2 * per_side * own // 16) * 16
    total = rows * (features // HEAD_SIZE)
    chunk = math.gcd(n, 16)
    anywhere = pl.BlockSpec(memory_space=pl.ANY)
    vector = pl.BlockSpec(memory_space=pltpu.VMEM)
    dma = pltpu.SemaphoreType.DMA
    results = (query, query, branch_key_value, turn_key_value, trunk)
    staged = pl.pallas_call(
        functools.partial(kernel, turn_count, branch_count),
        out_shape=tuple(pltpu.VMEM(a.shape, a.dtype) for a in results),
        in_specs=[anywhere] * 7,
        out_specs=(vector,) * 5,
        scratch_shapes=[
            pltpu.SMEM(branch_lengths.shape, jnp.int32),
            pltpu.SMEM(parents.shape, jnp.int32),
            pltpu.VMEM(query.shape, BF16),
            pltpu.VMEM(query.shape, BF16),
            pltpu.VMEM(branch_key_value.shape, BF16),
            pltpu.VMEM(turn_key_value.shape, BF16),
            pltpu.VMEM(trunk.shape, BF16),
            pltpu.VMEM((sides, slot, HEAD_SIZE), F32),
            pltpu.VMEM((sides, slot, HEAD_SIZE), BF16),
            pltpu.VMEM((sides, n * slot, HEAD_SIZE), BF16),
            pltpu.VMEM((sides, n * slot, HEAD_SIZE), BF16),
            pltpu.VMEM((sides, n * slot, HEAD_SIZE), BF16),
            pltpu.VMEM((2 * per_side, chunk * own, chunk * slot), BF16),
            pltpu.VMEM((2 * per_side, chunk * slot, chunk * own), BF16),
            pltpu.VMEM((rows, total), F32),
            pltpu.VMEM((rows, total), F32),
            pltpu.VMEM((1, total), F32),
            pltpu.VMEM((1, total), F32),
            pltpu.VMEM((1, total), F32),
            pltpu.VMEM((1, total), F32),
            pltpu.VMEM((1, total), F32),
            pltpu.VMEM((shared, total), BF16),
            pltpu.VMEM((shared, total), BF16),
            pltpu.VMEM((rows, rows), F32),
            pltpu.VMEM((shared, HEAD_SIZE), F32),
            pltpu.VMEM((shared, kv_width), BF16),
            pltpu.VMEM((shared, kv_width), BF16),
            dma((KEY_VALUE_HEADS,)),
            dma((KEY_VALUE_HEADS,)),
            dma((5,)),
            dma((2 * sides,)),
            dma((sides,)),
            dma((sides,)),
            dma((sides,)),
            dma((sides,)),
        ],
        compiler_params=pltpu.CompilerParams(
            collective_id=0, has_side_effects=True, vmem_limit_bytes=48 * 2**20
        ),
    )(
        *(
            pltpu.with_memory_space_constraint(a, pltpu.HBM)
            for a in (
                query, branch_key_value, turn_key_value, trunk, grad_out, branch_lengths, parents
            )
        )
    )
    outs = pl.pallas_call(
        put_out,
        out_shape=tuple(jax.ShapeDtypeStruct(a.shape, a.dtype) for a in results),
        in_specs=[vector] * 5,
        out_specs=(anywhere,) * 5,
        scratch_shapes=[dma((5,))],
        compiler_params=pltpu.CompilerParams(vmem_limit_bytes=2**20),
    )(*staged)
    return outs[:4] + (jnp.transpose(outs[4], (1, 0, 2)),)


def solution(mesh):
    every = ("parts", "turn", "branch")
    row = P(every, None)
    middle = P(None, every, None)
    return jax.shard_map(
        on_device,
        mesh=mesh,
        in_specs=(row, middle, middle, middle, row, row, P("parts")),
        out_specs=(row, row, middle, middle, middle),
        check_vma=False,
    )
```

time: 29.3 us -> 21.5 us (0.73)
  local copies, waits for them, and re-layouts: 7.29 us -> 0 us
  Pallas kernels: 21.1 us -> 20.7 us
    unnamed x13 -> x0, local copies, waits for them, and re-layouts: 6.71 us -> none
    pallas_call x1, Pallas kernels: 21.1 us -> 19.2 us  [on_device(): pl.pallas_call(functools.partial(kernel, turn_count, branch_count), out_s...]
    pallas_call x0 -> x1, Pallas kernels: none -> 1.44 us  [on_device(): pl.pallas_call(put_out, out_shape=tuple((jax.ShapeDtypeStruct(a.shape, a....]
    pallas_call x1 -> x0, local copies, waits for them, and re-layouts: 0.58 us -> none  [on_device(): pl.pallas_call(functools.partial(kernel, turn_count, branch_count), out_s...]
where the time goes in v2:
time: 21.5 us; the launch traced here: 21.3 us
  Pallas kernels  20.7 us (96%)
  between operations  0.64 us (3%)
    pallas_call x1, Pallas kernels, on_device(): pl.pallas_call(functools.partial(kernel, turn_count, branch_count), out_s...  19.2 us
    pallas_call x1, Pallas kernels, on_device(): pl.pallas_call(put_out, out_shape=tuple((jax.ShapeDtypeStruct(a.shape, a....  1.44 us

profile of v2, /device:TPU:0, one launch (start us, length us, event | category | flops | bytes accessed | tf_op | source)
XLA Modules:
  0.0 21.3 jit_solution(12941133050880615523)
XLA Ops:
  0.6 19.2 %shard_map.110 = (bf16[128,4096]{1,0:T(8,128)(2,1)S(1)}, bf16[128,4096]{1,0:T(8,128)(2,1)S(1)}, bf16[2,128,512]{2,1,0:T(8,128)(2,1)S(1)}, bf16[2,2,512]{2,1,0:T(2,128)(2,1)S(1)}, bf16[1,2,512]{2,1,0:T(2,128)(2,1)S(1)}) custom-call(bf16[128,4096]{1,0:T(8,128)(2,1)} %query.1, bf16[2,128,512]{2,1,0:T(8,128)(2,1)} %bkv.1, bf16[2,2,512]{2,1,0:T(2,128)(2,1)} %turn_kv.1, ...), custom_call_target="tpu_custom_call" | custom-call | tf_op jit(solution)/shard_map/pallas_call | solution.py:394
  19.9 1.4 %shard_map.111 = (bf16[128,4096]{1,0:T(8,128)(2,1)}, bf16[128,4096]{1,0:T(8,128)(2,1)}, bf16[2,128,512]{2,1,0:T(8,128)(2,1)}, bf16[2,2,512]{2,1,0:T(2,128)(2,1)}, bf16[1,2,512]{2,1,0:T(2,128)(2,1)}) custom-call(bf16[128,4096]{1,0:T(8,128)(2,1)S(1)} %get-tuple-element.15.refs_0_, bf16[128,4096]{1,0:T(8,128)(2,1)S(1)} %get-tuple-element.16.refs_1_, ...), custom_call_target="tpu_custom_call" | custom-call | tf_op jit(solution)/shard_map/pallas_call | solution.py:447
